TPU v7x, 32 devices: a whole 2x2x4 slice. The times are simulated.
32 devices in a mesh: vol: 8 (over z, x), rep: 4 (over y, core).
Axes of the slice: x: 2, y: 2, z: 4, core: 2. Of those that a mesh axis runs over, the one named last changes fastest.
Arguments:
- cutouts: bfloat16 [4, 256, 4096], P('rep', 'vol'), may hold values from -6 to 6
- counts: int32 [4, 8], P('rep', 'vol'), may hold values from 1 to 32, as said below
- partner: int32 [4, 128], P('rep'), may hold values from 0 to 127, as said below
- w_stem: bfloat16 [64, 128], replicated, may hold values from -0.75 to 0.75
- w_mix: bfloat16 [128, 128], replicated, may hold values from -0.5 to 0.5
- w_out: bfloat16 [128, 128], replicated, may hold values from -0.5 to 0.5
- w_proj: bfloat16 [128, 64], replicated, may hold values from -0.5 to 0.5
Outputs:
- upd_stem: float32 [64, 128], replicated
- upd_mix: float32 [128, 128], replicated
- upd_out: float32 [128, 128], replicated
- upd_proj: float32 [128, 64], replicated
- node_loss: float32 [4, 8, 16], P('rep', 'vol')
Inputs may be any that keep to these rules, and one draw needn't show every extreme that they name: `counts`: each row sums to 128, and its largest entry is exactly 32. Each row pairs the nodes of a group: partner[r, partner[r, g]] = g and partner[r, g] != g.
All inputs are finite; a program needn't handle non-finite values.
Results may differ from a plain program's by a relative error of at most 0.0035.
Values may be sent and summed in bfloat16 or wider, within the bound.
No kernel may reach another device: no remote copies, remote signals or barrier semaphores. Data moves between devices by JAX's collectives and lax.ppermute only.
A program may use at most 64 MiB of HBM per device.

v0:
```python
import jax
import jax.numpy as jnp
from jax import lax
from jax.sharding import PartitionSpec as P

logit_divisor_factor = 0.2
norm_eps = 1e-06
rms_eps = 1e-06


def prefix(part, axis, combine, identity):
    place = lax.axis_index(axis)
    gathered = lax.all_gather(part, axis)
    state = jnp.zeros_like(part) + jnp.asarray(identity, part.dtype)

    def one(lap, state):
        return combine(state, lax.dynamic_index_in_dim(gathered, lap, 0, False))

    return lax.fori_loop(0, place, one, state)


def first_dot(left, right):
    return lax.dot_general(
        left, right, (((0,), (0,)), ((), ())), preferred_element_type=jnp.float32
    )


def concluding_matrix_multiply(left, right):
    return lax.dot_general(
        left, right, (((1,), (1,)), ((), ())), preferred_element_type=jnp.float32
    )


def silu_slope(value):
    sigma = jax.nn.sigmoid(value)
    return sigma * (1.0 + value * (1.0 - sigma))


def encode(cutout_rows, w_stem, w_mix, w_out, w_proj):
    number = cutout_rows.shape[0]
    patches = cutout_rows.reshape(-1, w_stem.shape[0])
    per_cutout = patches.shape[0] // number
    pre_stem = jnp.dot(patches, w_stem, preferred_element_type=jnp.float32)
    hidden = jax.nn.silu(pre_stem).astype(jnp.bfloat16)
    pre_mix = jnp.dot(hidden, w_mix, preferred_element_type=jnp.float32)
    mixed = jax.nn.silu(pre_mix).astype(jnp.bfloat16)
    summed = hidden.astype(jnp.float32) + jnp.dot(mixed, w_out, preferred_element_type=jnp.float32)
    pooled = jnp.mean(summed.reshape(number, per_cutout, -1), axis=1).astype(jnp.bfloat16)
    raw_embed = jnp.dot(pooled, w_proj, preferred_element_type=jnp.float32)
    inv_norm = lax.rsqrt(jnp.sum(raw_embed * raw_embed, axis=1, keepdims=True) + norm_eps)
    unit_embed = raw_embed * inv_norm
    return (unit_embed, (patches, pre_stem, hidden, pre_mix, mixed, pooled, unit_embed, inv_norm))


def backward(feature_vector_derivative, saved, w_mix, w_out, w_proj):
    patches, pre_stem, hidden, pre_mix, mixed, pooled, unit_embed, inv_norm = saved
    number = pooled.shape[0]
    per_cutout = patches.shape[0] // number
    channels = hidden.shape[1]
    radial = jnp.sum(unit_embed * feature_vector_derivative, axis=1, keepdims=True)
    grad_raw = (inv_norm * (feature_vector_derivative - unit_embed * radial)).astype(jnp.bfloat16)
    grad_proj = first_dot(pooled, grad_raw)
    grad_pool = (concluding_matrix_multiply(grad_raw, w_proj) / per_cutout).astype(jnp.bfloat16)
    mixed_sum = jnp.sum(mixed.reshape(number, per_cutout, channels), axis=1, dtype=jnp.float32)
    grad_out = lax.dot_general(
        mixed_sum,
        grad_pool.astype(jnp.float32),
        (((0,), (0,)), ((), ())),
        precision=lax.Precision.HIGHEST,
        preferred_element_type=jnp.float32,
    )
    grad_mixed = concluding_matrix_multiply(grad_pool, w_out)
    mix_slope = silu_slope(pre_mix).reshape(number, per_cutout, channels)
    grad_pre_mix = (grad_mixed[:, None, :] * mix_slope).reshape(-1, channels).astype(jnp.bfloat16)
    grad_mix = first_dot(hidden, grad_pre_mix)
    spread_pool = jnp.broadcast_to(
        grad_pool.astype(jnp.float32)[:, None, :], (number, per_cutout, channels)
    ).reshape(-1, channels)
    grad_hidden = spread_pool + concluding_matrix_multiply(grad_pre_mix, w_mix)
    grad_pre_stem = (grad_hidden * silu_slope(pre_stem)).astype(jnp.bfloat16)
    grad_stem = first_dot(patches, grad_pre_stem)
    return (grad_stem, grad_mix, grad_out, grad_proj)


def contrast(anchor_feature_matrix, whole_feature_matrix, self_pos, pair_pos):
    cosine_affinity_matrix = (
        concluding_matrix_multiply(anchor_feature_matrix, whole_feature_matrix)
        / logit_divisor_factor
    )
    columns = lax.broadcasted_iota(jnp.int32, cosine_affinity_matrix.shape, 1)
    exp_scores = jnp.where(columns == self_pos[:, None], 0.0, jnp.exp(cosine_affinity_matrix))
    log_total = jnp.log(jnp.sum(exp_scores, axis=1))
    companion_feature_vector = jnp.take(whole_feature_matrix, pair_pos, axis=0).astype(jnp.float32)
    positive_couple_affinity = (
        jnp.sum(anchor_feature_matrix.astype(jnp.float32) * companion_feature_vector, axis=1)
        / logit_divisor_factor
    )
    return (exp_scores, log_total, companion_feature_vector, log_total - positive_couple_affinity)


def add_counts(earlier, later):
    return earlier + later


def locate(recv_ids, node_rank, slot_index):
    matches = recv_ids[None, :] == node_rank[:, None]
    from_slot = jnp.sum(jnp.where(matches, slot_index[None, :], 0), axis=1)
    return (matches, from_slot)


def on_device(cutouts, counts, partner, w_stem, w_mix, w_out, w_proj):
    vol_size = lax.axis_size("vol")
    vol_index = lax.axis_index("vol")
    max_nodes = cutouts.shape[1]
    node_dev = partner.shape[1] // vol_size
    capacity = (max_nodes + vol_size - 1) // vol_size
    own_cutouts = cutouts[0]
    own_count = counts[0, 0]
    offset = prefix(counts, "vol", add_counts, jnp.zeros_like(counts))[0, 0]
    slot_index = jnp.arange(vol_size * capacity, dtype=jnp.int32)
    target = slot_index // capacity
    first_rank = (offset - target + vol_size - 1) // vol_size
    slot_rank = first_rank + slot_index % capacity
    local_slot = slot_rank * vol_size + target - offset
    is_live = local_slot < own_count
    local_safe = jnp.clip(local_slot, 0, max_nodes - 1)
    send_ids = jnp.where(is_live, slot_rank, -1).astype(jnp.int32)
    node_rank = jnp.arange(node_dev, dtype=jnp.int32)
    packed = jnp.where(
        is_live[:, None], jnp.take(own_cutouts, local_safe, axis=0), jnp.zeros((), jnp.bfloat16)
    )
    arrived, recv_ids = (
        lax.all_to_all(packed, "vol", split_axis=0, concat_axis=0, tiled=True),
        lax.all_to_all(send_ids, "vol", split_axis=0, concat_axis=0, tiled=True),
    )
    matches, from_slot = locate(recv_ids, node_rank, slot_index)
    unit_embed, saved = encode(jnp.take(arrived, from_slot, axis=0), w_stem, w_mix, w_out, w_proj)
    anchor_feature_matrix = unit_embed.astype(jnp.bfloat16)
    whole_feature_matrix = lax.all_gather(anchor_feature_matrix, "vol", axis=0, tiled=True)
    self_pos = vol_index * node_dev + node_rank
    node_global = node_rank * vol_size + vol_index
    pair_global = jnp.take(partner[0], node_global)
    pair_pos = pair_global % vol_size * node_dev + pair_global // vol_size
    exp_scores, log_total, companion_feature_vector, node_loss = contrast(
        anchor_feature_matrix, whole_feature_matrix, self_pos, pair_pos
    )
    row_weight = (exp_scores * jnp.exp(-log_total)[:, None]).astype(jnp.bfloat16)
    horizontal_objective_term = jnp.dot(
        row_weight, whole_feature_matrix, preferred_element_type=jnp.float32
    )
    all_totals = lax.all_gather(log_total, "vol", axis=0, tiled=True)
    column_weight = (exp_scores * jnp.exp(-all_totals)[None, :]).astype(jnp.bfloat16)
    vertical_objective_term = jnp.dot(
        column_weight, whole_feature_matrix, preferred_element_type=jnp.float32
    )
    feature_vector_derivative = (
        horizontal_objective_term + vertical_objective_term - 2.0 * companion_feature_vector
    ) / logit_divisor_factor
    grads = backward(feature_vector_derivative, saved, w_mix, w_out, w_proj)
    grad_totals = lax.psum((grads[0], grads[1], grads[2], grads[3]), ("vol", "rep"))
    updates = [
        summed_grad * lax.rsqrt(jnp.mean(summed_grad * summed_grad) + rms_eps)
        for summed_grad in grad_totals
    ]
    return (updates[0], updates[1], updates[2], updates[3], node_loss[None, None, :])


def solution(mesh):
    in_specs = (P("rep", "vol", None), P("rep", "vol"), P("rep", None), P(), P(), P(), P())
    out_specs = (P(), P(), P(), P(), P("rep", "vol", None))
    return jax.shard_map(
        on_device, mesh=mesh, in_specs=in_specs, out_specs=out_specs, check_vma=False
    )
```

profile of v0, /device:TPU:0, one launch (start us, length us, event | category | flops | bytes accessed | tf_op | source)
XLA Modules:
  0.0 372.9 jit_solution(8634578186639433932)
XLA Ops:
  8.5 0.7 bitcast_dynamic-update-slice_fusion
  9.2 13.1 %all-reduce = s32[8]{0:T(128)S(1)} all-reduce(s32[8]{0:T(128)S(1)} %bitcast_dynamic-update-slice_fusion), channel_id=2, replica_groups=mesh['vol'=8,'rep'=4] {'vol'}, use_global_device_ids=true, to_apply=%add | all-reduce | flops 8 | bytes 64
  22.9 11.2 %all-to-all-start = ((s32[8,4,1]{1,2,0:T(1,128)}), s32[8,4,1]{1,2,0:T(1,128)S(1)}, u32[]{:S(2)}, u32[]{:S(2)}) async-start(s32[8,4,1]{1,2,0:T(1,128)} %compare_select_fusion), calls=%async_computation | async-start | bytes 8192 | tf_op jit(solution)/shard_map/all_to_all | solution.py:134
  34.2 0.6 copy-done.1
  34.8 0.7 gather_fusion.2
  35.6 0.7 gather_fusion
  36.5 0.9 select_select_fusion
  38.0 2.5 all-to-all-done
  40.6 3.5 all-to-all-start.1
  44.6 0.7 reduce.3
  45.7 6.6 %all-to-all-done.1 = bf16[8,4,4096]{2,1,0:T(4,128)(2,1)S(1)} async-done(((bf16[8,4,4096]{2,1,0:T(4,128)(2,1)}), bf16[8,4,4096]{2,1,0:T(4,128)(2,1)S(1)}, u32[]{:S(2)}, u32[]{:S(2)}) %all-to-all-start.1) | async-done | bytes 262176 | tf_op jit(solution)/shard_map/all_to_all | solution.py:133
  53.7 0.9 multiply_convert_fusion.1
  56.4 30.6 %all_gather.14 = bf16[128,64]{1,0:T(8,128)(2,1)S(1)} all-gather(bf16[16,64]{1,0:T(8,128)(2,1)S(1)} %multiply_convert_fusion.6), channel_id=1, replica_groups=mesh['vol'=8,'rep'=4] {'vol'}, dimensions={0}, use_global_device_ids=true | all-gather | bytes 18432 | tf_op jit(solution)/shard_map/all_gather | solution.py:139
  88.6 18.7 %all-reduce.1 = f32[128]{0:T(128)S(1)} all-reduce(f32[128]{0:T(128)S(1)} %get-tuple-element.60), channel_id=1, replica_groups=mesh['vol'=8,'rep'=4] {'vol'}, use_global_device_ids=true, to_apply=%add.1 | all-reduce | flops 128 | bytes 1024
  108.0 0.8 fusion.31
  109.2 0.9 fusion.51
  110.1 1.1 fusion.2
  111.3 0.9 fusion.52
  112.2 116.4 %all-reduce.7.cloned.1.call-done = (f32[64,128]{1,0:T(8,128)}, f32[128,64]{0,1:T(8,128)}) async-done(((f32[64,128]{1,0:T(8,128)}, f32[128,64]{0,1:T(8,128)}), (f32[64,128]{1,0:T(8,128)}, f32[128,64]{0,1:T(8,128)})) %all-reduce.7.cloned.1.call-update) | async-done | bytes 65552 | tf_op jit(solution)/shard_map/psum | solution.py:160
  228.6 1.4 multiply_reduce_fusion.2
  233.4 127.7 %all-reduce.9.cloned.1.call-done = (f32[128,128]{1,0:T(8,128)}, f32[128,128]{1,0:T(8,128)}) async-done(((f32[128,128]{1,0:T(8,128)}, f32[128,128]{1,0:T(8,128)}), (f32[128,128]{1,0:T(8,128)}, f32[128,128]{1,0:T(8,128)})) %all-reduce.9.cloned.1.call-update) | async-done | bytes 131088 | tf_op jit(solution)/shard_map/psum | solution.py:160
  361.1 1.5 multiply_reduce_fusion
  364.6 0.6 broadcast_multiply_fusion.1
  365.4 0.6 broadcast_multiply_fusion
  (72 shorter events, 11.0 us)
Async XLA Ops:
  7.2 28.5 %copy-start = (bf16[1,32,4096]{2,1,0:T(8,128)(2,1)S(1)}, bf16[1,32,4096]{2,1,0:T(8,128)(2,1)}, u32[]{:S(2)}) copy-start(bf16[1,32,4096]{2,1,0:T(8,128)(2,1)} %param.9) | copy-start | bytes 786436
  7.2 0.7 copy-start.10
  22.9 17.6 %all-to-all-start = ((s32[8,4,1]{1,2,0:T(1,128)}), s32[8,4,1]{1,2,0:T(1,128)S(1)}, u32[]{:S(2)}, u32[]{:S(2)}) async-start(s32[8,4,1]{1,2,0:T(1,128)} %compare_select_fusion), calls=%async_computation | async-start | bytes 8192 | tf_op jit(solution)/shard_map/all_to_all | solution.py:134
  34.2 0.7 copy-start.1
  40.6 11.7 %all-to-all-start.1 = ((bf16[8,4,4096]{2,1,0:T(4,128)(2,1)}), bf16[8,4,4096]{2,1,0:T(4,128)(2,1)S(1)}, u32[]{:S(2)}, u32[]{:S(2)}) async-start(bf16[8,4,4096]{2,1,0:T(4,128)(2,1)} %select_select_fusion), calls=%async_computation.1 | async-start | bytes 524288 | tf_op jit(solution)/shard_map/all_to_all | solution.py:133
  44.1 184.6 %all-reduce.7.cloned.1.call-start = ((), (), s32[]{:S(2)}) async-start(), calls=%async_computation.2 | async-start | bytes 131072 | tf_op jit(solution)/shard_map/psum | solution.py:160
  53.0 0.7 copy-start.9
  53.7 0.9 copy-start.8
  54.6 0.8 copy-start.7
  55.4 0.7 copy-start.6
  111.2 249.8 %all-reduce.9.cloned.1.call-start = ((), (), s32[]{:S(2)}) async-start(), calls=%async_computation.3 | async-start | bytes 262144 | tf_op jit(solution)/shard_map/psum | solution.py:160
  228.6 2.1 copy-start.5
  232.0 0.8 copy-start.4
  361.1 2.2 copy-start.3
  364.6 0.8 copy-start.2
Sparse Core Ops, SparseCore 0:
  111.4 117.2 all-reduce.6
  234.9 126.0 all-reduce.8
where the time goes:
time: 374 us; the launch traced here: 373 us
  waiting for transfers between devices  253 us (68%)
  blocking collectives  62.4 us (17%)
  between operations  18.4 us (5%)
  starting transfers between devices  14.8 us (4%)
  other arithmetic  10.2 us (3%)
  local copies, waits for them, and re-layouts  7.41 us (2%)
  matrix products  6.33 us (2%)
    psum x2, waiting for transfers between devices, on_device(): lax.psum((grads[0], grads[1], grads[2], grads[3]), ('vol', 'rep'))  244 us
    unnamed x2, blocking collectives  31.8 us
    all_gather x1, blocking collectives, on_device(): lax.all_gather(anchor_feature_matrix, 'vol', axis=0, tiled=True)  30.6 us
    all_to_all x1, starting transfers between devices, on_device(): lax.all_to_all(send_ids, 'vol', split_axis=0, concat_axis=0, tiled=True)  11.2 us
  transfers between devices with their start and end apart: 4, of which 4 were waited for; matrix products, arithmetic and copies ran while one was open for 2% of the time, Pallas kernels for 0%

commit v1 on v0

--- a/solution.py
+++ b/solution.py
@@ -157,7 +157,7 @@
         horizontal_objective_term + vertical_objective_term - 2.0 * companion_feature_vector
     ) / logit_divisor_factor
     grads = backward(feature_vector_derivative, saved, w_mix, w_out, w_proj)
-    grad_totals = lax.psum((grads[0], grads[1], grads[2], grads[3]), ("vol", "rep"))
+    grad_totals = lax.psum(lax.psum((grads[0], grads[1], grads[2], grads[3]), "vol"), "rep")
     updates = [
         summed_grad * lax.rsqrt(jnp.mean(summed_grad * summed_grad) + rms_eps)
         for summed_grad in grad_totals

time: 374 us -> 332 us (0.89)
  waiting for transfers between devices: 253 us -> 211 us
    psum x2 -> x4, waiting for transfers between devices: 244 us -> 201 us  [the longest x2 137 us: on_device(): lax.psum((grads[0], grads[1], grads[2], grads[3]), 'vol')]
  transfers between devices with their start and end apart: 4 -> 6, of which waited for: 4 -> 6; matrix products, arithmetic and copies ran while one was open for 2% -> 3% of each run, Pallas kernels for 0% -> 0%
where the time goes in v1:
time: 332 us; the launch traced here: 331 us
  waiting for transfers between devices  211 us (64%)
  blocking collectives  62.4 us (19%)
  between operations  18.2 us (5%)
  starting transfers between devices  14.9 us (4%)
  other arithmetic  10.2 us (3%)
  local copies, waits for them, and re-layouts  8.01 us (2%)
  matrix products  6.33 us (2%)
    psum x2, waiting for transfers between devices, on_device(): lax.psum((grads[0], grads[1], grads[2], grads[3]), 'vol')  137 us
    psum x2, waiting for transfers between devices, on_device(): lax.psum(lax.psum((grads[0], grads[1], grads[2], grads[3]), 'vol'), 'rep')  64.7 us
    unnamed x2, blocking collectives  31.8 us
    all_gather x1, blocking collectives, on_device(): lax.all_gather(anchor_feature_matrix, 'vol', axis=0, tiled=True)  30.6 us
    all_to_all x1, starting transfers between devices, on_device(): lax.all_to_all(send_ids, 'vol', split_axis=0, concat_axis=0, tiled=True)  11.2 us
  transfers between devices with their start and end apart: 6, of which 6 were waited for; matrix products, arithmetic and copies ran while one was open for 3% of the time, Pallas kernels for 0%

profile of v1, /device:TPU:0, one launch (start us, length us, event | category | flops | bytes accessed | tf_op | source)
XLA Modules:
  0.0 330.7 jit_solution(12899031979449577498)
XLA Ops:
  8.5 0.7 bitcast_dynamic-update-slice_fusion
  9.2 13.1 %all-reduce = s32[8]{0:T(128)S(1)} all-reduce(s32[8]{0:T(128)S(1)} %bitcast_dynamic-update-slice_fusion), channel_id=2, replica_groups=mesh['vol'=8,'rep'=4] {'vol'}, use_global_device_ids=true, to_apply=%add | all-reduce | flops 8 | bytes 64
  22.9 11.2 %all-to-all-start = ((s32[8,4,1]{1,2,0:T(1,128)}), s32[8,4,1]{1,2,0:T(1,128)S(1)}, u32[]{:S(2)}, u32[]{:S(2)}) async-start(s32[8,4,1]{1,2,0:T(1,128)} %compare_select_fusion), calls=%async_computation | async-start | bytes 8192 | tf_op jit(solution)/shard_map/all_to_all | solution.py:134
  34.8 0.7 gather_fusion.2
  35.6 0.7 gather_fusion
  36.5 0.9 select_select_fusion
  38.0 2.5 all-to-all-done
  40.6 3.5 %all-to-all-start.1 = ((bf16[8,4,4096]{2,1,0:T(4,128)(2,1)}), bf16[8,4,4096]{2,1,0:T(4,128)(2,1)S(1)}, u32[]{:S(2)}, u32[]{:S(2)}) async-start(bf16[8,4,4096]{2,1,0:T(4,128)(2,1)} %select_select_fusion), calls=%async_computation.1 | async-start | bytes 524288 | tf_op jit(solution)/shard_map/all_to_all | solution.py:133
  44.6 0.7 reduce.3
  45.7 6.6 %all-to-all-done.1 = bf16[8,4,4096]{2,1,0:T(4,128)(2,1)S(1)} async-done(((bf16[8,4,4096]{2,1,0:T(4,128)(2,1)}), bf16[8,4,4096]{2,1,0:T(4,128)(2,1)S(1)}, u32[]{:S(2)}, u32[]{:S(2)}) %all-to-all-start.1) | async-done | bytes 262176 | tf_op jit(solution)/shard_map/all_to_all | solution.py:133
  53.7 0.9 multiply_convert_fusion.1
  56.4 30.6 %all_gather.14 = bf16[128,64]{1,0:T(8,128)(2,1)S(1)} all-gather(bf16[16,64]{1,0:T(8,128)(2,1)S(1)} %multiply_convert_fusion.6), channel_id=1, replica_groups=mesh['vol'=8,'rep'=4] {'vol'}, dimensions={0}, use_global_device_ids=true | all-gather | bytes 18432 | tf_op jit(solution)/shard_map/all_gather | solution.py:139
  88.6 18.7 %all-reduce.1 = f32[128]{0:T(128)S(1)} all-reduce(f32[128]{0:T(128)S(1)} %get-tuple-element.64), channel_id=1, replica_groups=mesh['vol'=8,'rep'=4] {'vol'}, use_global_device_ids=true, to_apply=%add.1 | all-reduce | flops 128 | bytes 1024
  108.0 0.8 fusion.31
  109.2 1.1 fusion.2
  110.4 0.9 fusion.51
  111.3 66.0 %all-reduce.11.cloned.1.call-done = (f32[64,128]{1,0:T(8,128)}, f32[128,64]{0,1:T(8,128)}) async-done(((f32[64,128]{1,0:T(8,128)}, f32[128,64]{0,1:T(8,128)}), (f32[64,128]{1,0:T(8,128)}, f32[128,64]{0,1:T(8,128)})) %all-reduce.11.cloned.1.call-update) | async-done | bytes 65552 | tf_op jit(solution)/shard_map/psum | solution.py:160
  177.4 0.9 fusion.52
  178.3 32.9 %all-reduce.15.cloned.1.call-done = (f32[64,128]{1,0:T(8,128)}, f32[128,64]{0,1:T(8,128)}) async-done(((f32[64,128]{1,0:T(8,128)}, f32[128,64]{0,1:T(8,128)}), (f32[64,128]{1,0:T(8,128)}, f32[128,64]{0,1:T(8,128)})) %all-reduce.15.cloned.1.call-update) | async-done | bytes 65552 | tf_op jit(solution)/shard_map/psum | solution.py:160
  211.2 1.4 multiply_reduce_fusion.2
  215.2 70.8 %all-reduce.13.cloned.1.call-done = (f32[128,128]{1,0:T(8,128)}, f32[128,128]{1,0:T(8,128)}) async-done(((f32[128,128]{1,0:T(8,128)}, f32[128,128]{1,0:T(8,128)}), (f32[128,128]{1,0:T(8,128)}, f32[128,128]{1,0:T(8,128)})) %all-reduce.13.cloned.1.call-update) | async-done | bytes 131088 | tf_op jit(solution)/shard_map/psum | solution.py:160
  286.0 0.7 copy-done.4
  287.4 31.8 %all-reduce.17.cloned.1.call-done = (f32[128,128]{1,0:T(8,128)}, f32[128,128]{1,0:T(8,128)}) async-done(((f32[128,128]{1,0:T(8,128)}, f32[128,128]{1,0:T(8,128)}), (f32[128,128]{1,0:T(8,128)}, f32[128,128]{1,0:T(8,128)})) %all-reduce.17.cloned.1.call-update) | async-done | bytes 131088 | tf_op jit(solution)/shard_map/psum | solution.py:160
  319.2 1.5 multiply_reduce_fusion
  (78 shorter events, 12.9 us)
Async XLA Ops:
  7.2 28.5 %copy-start = (bf16[1,32,4096]{2,1,0:T(8,128)(2,1)S(1)}, bf16[1,32,4096]{2,1,0:T(8,128)(2,1)}, u32[]{:S(2)}) copy-start(bf16[1,32,4096]{2,1,0:T(8,128)(2,1)} %param.9) | copy-start | bytes 786436
  7.2 0.7 copy-start.10
  22.9 17.6 %all-to-all-start = ((s32[8,4,1]{1,2,0:T(1,128)}), s32[8,4,1]{1,2,0:T(1,128)S(1)}, u32[]{:S(2)}, u32[]{:S(2)}) async-start(s32[8,4,1]{1,2,0:T(1,128)} %compare_select_fusion), calls=%async_computation | async-start | bytes 8192 | tf_op jit(solution)/shard_map/all_to_all | solution.py:134
  34.2 0.7 copy-start.1
  40.6 11.7 %all-to-all-start.1 = ((bf16[8,4,4096]{2,1,0:T(4,128)(2,1)}), bf16[8,4,4096]{2,1,0:T(4,128)(2,1)S(1)}, u32[]{:S(2)}, u32[]{:S(2)}) async-start(bf16[8,4,4096]{2,1,0:T(4,128)(2,1)} %select_select_fusion), calls=%async_computation.1 | async-start | bytes 524288 | tf_op jit(solution)/shard_map/all_to_all | solution.py:133
  44.1 133.2 %all-reduce.11.cloned.1.call-start = ((), (), s32[]{:S(2)}) async-start(), calls=%async_computation.2 | async-start | bytes 131072 | tf_op jit(solution)/shard_map/psum | solution.py:160
  53.0 0.7 copy-start.9
  53.7 0.9 copy-start.8
  54.6 0.8 copy-start.7
  55.4 0.7 copy-start.6
  110.3 100.9 %all-reduce.15.cloned.1.call-start = ((), (), s32[]{:S(2)}) async-start(), calls=%async_computation.4 | async-start | bytes 131072 | tf_op jit(solution)/shard_map/psum | solution.py:160
  177.3 108.7 %all-reduce.13.cloned.1.call-start = ((), (), s32[]{:S(2)}) async-start(), calls=%async_computation.3 | async-start | bytes 262144 | tf_op jit(solution)/shard_map/psum | solution.py:160
  178.3 140.9 %all-reduce.17.cloned.1.call-start = ((), (), s32[]{:S(2)}) async-start(), calls=%async_computation.5 | async-start | bytes 262144 | tf_op jit(solution)/shard_map/psum | solution.py:160
  211.2 2.1 copy-start.5
  286.0 0.8 copy-start.4
  319.2 2.2 copy-start.3
  322.7 0.8 copy-start.2
Sparse Core Ops, SparseCore 0:
  110.5 66.7 all-reduce.10
  179.7 31.4 all-reduce.14
  215.3 70.6 all-reduce.12
  288.2 30.9 all-reduce.16
